TPU v7x, 256 devices: a whole 4x4x8 slice. The times are simulated.
256 devices in a mesh: row: 16 (over y_hi, x, core), col: 16 (over z, y_lo).
Axes of the slice: x: 4, y: 4 (y_hi: 2, y_lo: 2; y = y_hi * 2 + y_lo), z: 8, core: 2. Of those that a mesh axis runs over, the one named last changes fastest.
Arguments:
- hessenberg: float32 [16384, 16384], P('row', 'col'), may hold values from -6 to 6, as said below
- factors: float32 [3, 32, 512, 512], P(None, 'row', 'col'), may hold values from -1 to 1, as said below
- active: int32 [3, 32], replicated, may hold values 0 or 1
Outputs:
- updated_slab: float32 [16384, 16384], P('row', 'col')
Inputs may be any that keep to these rules, and one draw needn't show every extreme that they name: `hessenberg`: in global order, zero below the first subdiagonal. Each factors[f, s] is orthogonal up to float32 rounding.
All inputs are finite; a program needn't handle non-finite values.
Results may differ from a plain program's by a relative error of at most 0.0001.
Values sent between devices are 32-bit elements; how exact they have to be, the bound alone decides.
A program may use at most 64 MiB of HBM per device.

v0:
```python
import jax
import jax.numpy as jnp
from jax import lax
from jax.sharding import PartitionSpec as P

PRECISE = lax.Precision.HIGHEST


def passed_along(value, axis, steps):
    count = lax.axis_size(axis)
    pairs = [(source, (source + steps) % count) for source in range(count)]
    return lax.ppermute(value, axis, pairs)


def left_apply(factor, stacked):
    return jnp.einsum("kab,kan->kbn", factor, stacked, precision=PRECISE)


def right_apply(stacked, factor):
    return jnp.einsum("nka,kab->nkb", stacked, factor, precision=PRECISE)


def effective(factor, flag_row):
    identity = jnp.eye(factor.shape[-1], dtype=jnp.float32)
    return jnp.where(flag_row[:, None, None] > 0, factor, identity)


def wrap_fix(received, at_edge, offset_by, along_dim):
    return jnp.where(at_edge, jnp.roll(received, offset_by, axis=along_dim), received)


def sort_columns(collected, grid_rows):
    phases, all_blocks, pieces, window = collected.shape
    natural = collected.reshape(
        phases, grid_rows, all_blocks // grid_rows, pieces, window
    ).transpose(0, 2, 1, 3, 4)
    return natural.transpose(0, 2, 1, 3, 4)


def local(hessenberg, factors, active):
    rows_here, cols_here = hessenberg.shape
    window = factors.shape[-1]
    half_win = window // 2
    phases = factors.shape[0]
    grid_rows = lax.axis_size("row")
    grid_cols = lax.axis_size("col")
    row_index = lax.axis_index("row")
    col_index = lax.axis_index("col")
    row_blocks = rows_here // window
    col_blocks = cols_here // window
    all_blocks = row_blocks * grid_rows
    slot_row = jnp.arange(row_blocks, dtype=jnp.int32) * grid_rows + row_index
    slot_col = jnp.arange(col_blocks, dtype=jnp.int32) * grid_cols + col_index
    within = jnp.arange(window, dtype=jnp.int32)
    glob_row = (slot_row[:, None] * window + within[None, :]).reshape(rows_here)
    glob_col = (slot_col[:, None] * window + within[None, :]).reshape(cols_here)
    current = hessenberg
    for phase_idx in range(phases):
        chosen = factors[phase_idx : phase_idx + 1]
        row_raw = lax.all_gather(chosen, "col", axis=2, tiled=True)[0]
        gathered = lax.all_gather(chosen, "row", axis=1, tiled=True)
        col_raw = lax.all_to_all(
            sort_columns(gathered, grid_rows), "col", split_axis=1, concat_axis=3, tiled=True
        )
        col_raw = col_raw.reshape(col_blocks, window, window)
        flag_all = active[phase_idx]
        row_flag = jnp.take(flag_all, slot_row)
        col_flag = jnp.take(flag_all, slot_col)
        if phase_idx % 2 == 1:
            row_flag = jnp.where(slot_row < all_blocks - 1, row_flag, 0)
            col_flag = jnp.where(slot_col < all_blocks - 1, col_flag, 0)
        row_factor = effective(row_raw, row_flag)
        col_factor = effective(col_raw, col_flag)
        blocks = current.reshape(row_blocks, window, cols_here)
        if phase_idx % 2 == 0:
            updated = left_apply(row_factor, blocks)
            keep_mask = glob_col[None, :] >= (slot_row[:, None] + 1) * window
            current = jnp.where(keep_mask[:, None, :], updated, blocks).reshape(
                rows_here, cols_here
            )
            columns = current.reshape(rows_here, col_blocks, window)
            updated = right_apply(columns, col_factor)
            keep_mask = glob_row[:, None] < slot_col[None, :] * window
            current = jnp.where(keep_mask[:, :, None], updated, columns).reshape(
                rows_here, cols_here
            )
        else:
            top_half = blocks[:, :half_win]
            bottoms = blocks[:, half_win:]
            from_below = wrap_fix(
                passed_along(top_half, "row", -1), row_index == grid_rows - 1, -1, 0
            )
            stacked = jnp.concatenate([bottoms, from_below], axis=1)
            updated = left_apply(row_factor, stacked)
            keep_mask = glob_col[None, :] >= slot_row[:, None] * window + window + half_win
            updated = jnp.where(keep_mask[:, None, :], updated, stacked)
            returned = wrap_fix(passed_along(updated[:, half_win:], "row", 1), row_index == 0, 1, 0)
            current = jnp.concatenate([returned, updated[:, :half_win]], axis=1).reshape(
                rows_here, cols_here
            )
            columns = current.reshape(rows_here, col_blocks, window)
            left_half = columns[:, :, :half_win]
            right_half = columns[:, :, half_win:]
            from_right = wrap_fix(
                passed_along(left_half, "col", -1), col_index == grid_cols - 1, -1, 1
            )
            stacked = jnp.concatenate([right_half, from_right], axis=2)
            updated = right_apply(stacked, col_factor)
            keep_mask = glob_row[:, None] < slot_col[None, :] * window + half_win
            updated = jnp.where(keep_mask[:, :, None], updated, stacked)
            returned = wrap_fix(
                passed_along(updated[:, :, half_win:], "col", 1), col_index == 0, 1, 1
            )
            current = jnp.concatenate([returned, updated[:, :, :half_win]], axis=2).reshape(
                rows_here, cols_here
            )
    return current


def solution(mesh):
    return jax.shard_map(
        local,
        mesh=mesh,
        in_specs=(P("row", "col"), P(None, "row", "col", None), P()),
        out_specs=P("row", "col"),
        check_vma=False,
    )
```

profile of v0, /device:TPU:6, one launch (start us, length us, event | category | flops | bytes accessed | tf_op | source)
XLA Modules:
  0.0 637.7 jit_solution(7800001573734973021)
XLA Ops:
  6.5 1.9 slice_bitcast_fusion
  8.5 0.7 all-gather.17.cloned.1.call-update
  9.2 57.1 %all-gather.15.cloned.1.call-done = f32[1,32,32,512]{3,2,0,1:T(8,128)} async-done(((f32[1,2,32,512]{3,2,0,1:T(8,128)}), f32[1,32,32,512]{3,2,0,1:T(8,128)}) %all-gather.15.cloned.1.call-update) | async-done | bytes 2097168 | tf_op jit(solution)/shard_map/all_gather | solution.py:61
  66.3 7.3 %all-to-all-start.2 = ((f32[1,16,2,32,512]{4,3,2,0,1:T(8,128)}), f32[1,16,2,32,512]{4,3,2,0,1:T(8,128)S(1)}, u32[]{:S(2)}, u32[]{:S(2)}) async-start(f32[1,16,2,32,512]{4,3,2,0,1:T(8,128)} %bitcast.71), calls=%async_computation.2 | async-start | bytes 4194304 | tf_op jit(solution)/shard_map/all_to_all | solution.py:62
  73.6 0.7 all-gather.13.cloned.1.call-update
  74.6 0.6 gather_fusion.5
  75.2 0.6 gather_fusion.4
  76.2 91.1 %all-gather.17.cloned.1.call-done = f32[1,2,512,512]{3,2,1,0:T(8,128)} async-done(((f32[1,2,32,512]{3,2,1,0:T(8,128)}), f32[1,2,512,512]{3,2,1,0:T(8,128)}) %all-gather.17.cloned.1.call-update) | async-done | bytes 2097168 | tf_op jit(solution)/shard_map/all_gather | solution.py:60
  167.3 11.6 %convolution_select_fusion.1 = f32[2,512,1024]{2,1,0:T(8,128)} fusion(f32[2,512,1024]{2,1,0:T(8,128)} %bitcast.69, f32[1,2,512,512]{3,2,1,0:T(8,128)} %all-gather.17.cloned.1.call-done, pred[2,1024]{1,0:T(4,128)(4,1)S(1)} %get-tuple-element.30, f32[512,512]{1,0:T(8,128)S(1)} %fusion.20, pred[2]{0:T(512)(128)(4,1)S(1)} %select_compare_fusion), kind=kOutput, calls=%fused_computation.17 | convolution fusion | flops 6444023808 | bytes 11536386 | tf_op jit(solution)/shard_map/kab,kan->kbn/dot_general | solution.py:16
  178.9 6.6 %reshape_reshape.15 = f32[1024,2,512]{2,1,0:T(2,128)} reshape(f32[2,512,1024]{2,1,0:T(8,128)} %convolution_select_fusion.1) | data formatting | bytes 8388608 | tf_op jit(solution)/shard_map/reshape;reshape | solution.py:81
  185.5 7.2 %copy.56 = f32[1024,2,512]{0,2,1:T(8,128)} copy(f32[1024,2,512]{2,1,0:T(2,128)} %reshape_reshape.15) | data formatting | bytes 8388608 | tf_op jit(solution)/shard_map/reshape;reshape | solution.py:81
  192.7 0.2 copy.52
  192.9 2.0 copy-done
  194.9 8.8 %bitcast_select_fusion.2 = f32[1024,2,512]{0,2,1:T(8,128)} fusion(f32[1024,2,512]{0,2,1:T(8,128)S(1)} %copy-done, f32[2,512,512]{2,1,0:T(8,128)S(1)} %bitcast.67, pred[1024,2]{0,1:T(4,128)(4,1)S(1)} %get-tuple-element.28, f32[512,512]{1,0:T(8,128)S(1)} %fusion.20, pred[2]{0:T(512)(128)(4,1)S(1)} %select_compare_fusion.1), kind=kOutput, calls=%fused_computation.12 | convolution fusion | flops 6444023808 | bytes 11536386 | tf_op jit(solution)/shard_map/nka,kab->nkb/dot_general | solution.py:20
  203.7 6.6 %reshape_reshape.16 = f32[2,512,1024]{1,0,2:T(2,128)} reshape(f32[1024,2,512]{0,2,1:T(8,128)} %bitcast_select_fusion.2) | data formatting | bytes 8388608 | tf_op jit(solution)/shard_map/reshape;reshape | solution.py:74
  210.3 5.0 fusion.30
  215.3 2.9 copy.79
  218.2 0.2 collective-permute-start
  218.4 0.6 gather_fusion.3
  219.1 4.1 copy.78
  223.2 19.0 %collective-permute-done = f32[2,256,1024]{2,1,0:T(8,128)S(1)} collective-permute-done((f32[2,256,1024]{2,1,0:T(8,128)}, f32[2,256,1024]{2,1,0:T(8,128)S(1)}, u32[]{:S(2)}, u32[]{:S(2)}) %collective-permute-start) | collective-permute-done | bytes 2097184 | tf_op jit(solution)/shard_map/ppermute | solution.py:12
  242.3 1.2 copy-done.1
  243.5 1.8 maximum_select_fusion
  245.4 18.9 %all-gather.13.cloned.1.call-done = f32[1,2,512,512]{3,2,1,0:T(8,128)} async-done(((f32[1,2,32,512]{3,2,1,0:T(8,128)}), f32[1,2,512,512]{3,2,1,0:T(8,128)}) %all-gather.13.cloned.1.call-update) | async-done | bytes 2097168 | tf_op jit(solution)/shard_map/all_gather | solution.py:60
  264.3 10.6 %fusion.1 = f32[2,512,1024]{2,1,0:T(8,128)S(1)} fusion(f32[2,256,1024]{2,1,0:T(8,128)S(1)} %maximum_select_fusion, f32[2,256,1024]{2,1,0:T(8,128)} %copy.78, pred[2,1024]{1,0:T(4,128)(4,1)S(1)} %get-tuple-element.29, f32[1,2,512,512]{3,2,1,0:T(8,128)} %all-gather.13.cloned.1.call-done, f32[512,512]{1,0:T(8,128)S(1)} %fusion.20, pred[2]{0:T(512)(128)(4,1)S(1)} %fusion.22), kind=kOutput, calls=%fused_computation.14 | convolution fusion | flops 6446120960 | bytes 11536386 | tf_op jit(solution)/shard_map/kab,kan->kbn/dot_general | solution.py:16
  274.9 2.3 fusion.29
  277.3 44.1 %all-gather.11.cloned.1.call-done = f32[1,32,32,512]{3,2,0,1:T(8,128)} async-done(((f32[1,2,32,512]{3,2,0,1:T(8,128)}), f32[1,32,32,512]{3,2,0,1:T(8,128)}) %all-gather.11.cloned.1.call-update) | async-done | bytes 2097168 | tf_op jit(solution)/shard_map/all_gather | solution.py:61
  321.4 7.6 %all-to-all-start.1 = ((f32[1,16,2,32,512]{4,3,2,0,1:T(8,128)}), f32[1,16,2,32,512]{4,3,2,0,1:T(8,128)}, u32[]{:S(2)}, u32[]{:S(2)}) async-start(f32[1,16,2,32,512]{4,3,2,0,1:T(8,128)} %bitcast.72), calls=%async_computation.1 | async-start | bytes 4194304 | tf_op jit(solution)/shard_map/all_to_all | solution.py:62
  329.0 0.1 fusion.33
  329.2 0.4 maximum_select_fusion.1
  329.6 1.2 copy-done.4
  330.8 2.5 pad_maximum_fusion.1
  333.3 6.6 %reshape_reshape.17 = f32[1024,2,512]{2,1,0:T(2,128)} reshape(f32[2,512,1024]{2,1,0:T(8,128)} %pad_maximum_fusion.1) | data formatting | bytes 8388608 | tf_op jit(solution)/shard_map/reshape;reshape | solution.py:101
  339.9 5.0 fusion.28
  344.9 1.5 copy.81
  346.4 4.1 collective-permute-start.2
  350.5 85.0 %all-gather.7.cloned.1.call-done = f32[1,32,32,512]{3,2,0,1:T(8,128)} async-done(((f32[1,2,32,512]{3,2,0,1:T(8,128)}), f32[1,32,32,512]{3,2,0,1:T(8,128)}) %all-gather.7.cloned.1.call-update) | async-done | bytes 2097168 | tf_op jit(solution)/shard_map/all_gather | solution.py:61
  435.5 6.6 %all-to-all-start = ((f32[1,16,2,32,512]{4,3,2,0,1:T(8,128)}), f32[1,16,2,32,512]{4,3,2,0,1:T(8,128)}, u32[]{:S(2)}, u32[]{:S(2)}) async-start(f32[1,16,2,32,512]{4,3,2,0,1:T(8,128)} %bitcast.70), calls=%async_computation | async-start | bytes 4194304 | tf_op jit(solution)/shard_map/all_to_all | solution.py:62
  442.1 0.5 all-gather.9.cloned.1.call-update
  442.7 0.6 gather_fusion.2
  443.3 2.0 copy.49
  445.4 0.2 copy-done.3
  445.6 0.2 copy.80
  445.7 0.1 fusion.32
  445.9 0.3 maximum_select_fusion.2
  446.2 7.8 %bitcast_select_fusion.1 = f32[1024,2,512]{2,0,1:T(8,128)S(1)} fusion(f32[1024,2,256]{2,0,1:T(8,128)S(1)} %maximum_select_fusion.2, f32[1024,2,256]{2,0,1:T(8,128)S(1)} %copy.80, pred[1024,2]{0,1:T(4,128)(4,1)S(1)} %get-tuple-element.27, f32[2,512,512]{2,1,0:T(8,128)S(1)} %bitcast.68, f32[512,512]{1,0:T(8,128)S(1)} %fusion.20, pred[2]{0:T(512)(128)(4,1)S(1)} %fusion.21), kind=kOutput, calls=%fused_computation.11 | convolution fusion | flops 6446120960 | bytes 11536386 | tf_op jit(solution)/shard_map/nka,kab->nkb/dot_general | solution.py:20
  453.9 2.4 fusion.27
  456.3 2.0 collective-permute-start.3
  458.4 0.6 gather_fusion.1
  459.0 0.6 gather_fusion
  459.7 36.5 %all-to-all-done = f32[1,16,2,32,512]{4,3,2,0,1:T(8,128)} async-done(((f32[1,16,2,32,512]{4,3,2,0,1:T(8,128)}), f32[1,16,2,32,512]{4,3,2,0,1:T(8,128)}, u32[]{:S(2)}, u32[]{:S(2)}) %all-to-all-start) | async-done | bytes 2097184 | tf_op jit(solution)/shard_map/all_to_all | solution.py:62
  496.1 3.3 copy.46
  499.4 49.3 %collective-permute-done.3 = f32[1024,2,256]{2,0,1:T(8,128)S(1)} collective-permute-done((f32[1024,2,256]{2,0,1:T(8,128)}, f32[1024,2,256]{2,0,1:T(8,128)S(1)}, u32[]{:S(2)}, u32[]{:S(2)}) %collective-permute-start.3) | collective-permute-done | bytes 2097184 | tf_op jit(solution)/shard_map/ppermute | solution.py:12
  548.9 0.4 maximum_select_fusion.3
  549.3 1.2 copy-done.5
  550.5 0.6 pad_maximum_fusion.3
  551.1 5.3 copy.64
  556.4 6.6 %reshape_reshape.18 = f32[2,512,1024]{2,1,0:T(8,128)} reshape(f32[1024,2,512]{2,1,0:T(2,128)} %copy.64) | data formatting | bytes 8388608 | tf_op jit(solution)/shard_map/reshape;reshape | solution.py:74
  563.0 25.0 %all-gather.9.cloned.1.call-done = f32[1,2,512,512]{3,2,0,1:T(8,128)} async-done(((f32[1,2,32,512]{3,2,0,1:T(8,128)}), f32[1,2,512,512]{3,2,0,1:T(8,128)}) %all-gather.9.cloned.1.call-update) | async-done | bytes 2097168 | tf_op jit(solution)/shard_map/all_gather | solution.py:60
  587.9 11.6 %convolution_select_fusion = f32[2,512,1024]{2,1,0:T(8,128)} fusion(f32[2,512,1024]{2,1,0:T(8,128)} %reshape_reshape.18, f32[1,2,512,512]{3,2,0,1:T(8,128)} %all-gather.9.cloned.1.call-done, pred[2,1024]{1,0:T(4,128)(4,1)S(1)} %get-tuple-element.30, f32[512,512]{1,0:T(8,128)S(1)} %fusion.20, pred[2]{0:T(512)(128)(4,1)S(1)} %select_compare_fusion.2), kind=kOutput, calls=%fused_computation.16 | convolution fusion | flops 6444023808 | bytes 11536386 | tf_op jit(solution)/shard_map/kab,kan->kbn/dot_general | solution.py:16
  599.5 6.6 %reshape_reshape.19 = f32[1024,2,512]{2,1,0:T(2,128)} reshape(f32[2,512,1024]{2,1,0:T(8,128)} %convolution_select_fusion) | data formatting | bytes 8388608 | tf_op jit(solution)/shard_map/reshape;reshape | solution.py:81
  606.1 7.3 %copy.68 = f32[1024,2,512]{0,2,1:T(8,128)} copy(f32[1024,2,512]{2,1,0:T(2,128)} %reshape_reshape.19) | data formatting | bytes 8388608 | tf_op jit(solution)/shard_map/reshape;reshape | solution.py:81
  613.4 11.9 %bitcast_select_fusion = f32[1024,2,512]{0,2,1:T(8,128)} fusion(f32[1024,2,512]{0,2,1:T(8,128)} %copy.68, f32[2,512,512]{2,1,0:T(8,128)S(1)} %bitcast.66, pred[1024,2]{0,1:T(4,128)(4,1)S(1)} %get-tuple-element.28, f32[512,512]{1,0:T(8,128)S(1)} %fusion.20, pred[2]{0:T(512)(128)(4,1)S(1)} %select_compare_fusion.3), kind=kOutput, calls=%fused_computation.10 | convolution fusion | flops 6444023808 | bytes 11536386 | tf_op jit(solution)/shard_map/nka,kab->nkb/dot_general | solution.py:20
  625.3 5.3 copy.69
  (45 shorter events, 1.1 us)
Async XLA Ops:
  6.5 59.7 %all-gather.15.cloned.1.call-start = ((), (), s32[]{:S(2)}) async-start(), calls=%async_computation.7 | async-start | bytes 2228224 | tf_op jit(solution)/shard_map/all_gather | solution.py:61
  8.4 158.9 %all-gather.17.cloned.1.call-start = ((), (), s32[]{:S(2)}) async-start(), calls=%async_computation.8 | async-start | bytes 2228224 | tf_op jit(solution)/shard_map/all_gather | solution.py:60
  66.3 8.3 %copy-start.6 = (s32[3,32]{1,0:T(4,128)S(1)}, s32[3,32]{1,0:T(4,128)}, u32[]{:S(2)}) copy-start(s32[3,32]{1,0:T(4,128)} %param.7) | copy-start | bytes 1156
  66.3 126.4 %all-to-all-start.2 = ((f32[1,16,2,32,512]{4,3,2,0,1:T(8,128)}), f32[1,16,2,32,512]{4,3,2,0,1:T(8,128)S(1)}, u32[]{:S(2)}, u32[]{:S(2)}) async-start(f32[1,16,2,32,512]{4,3,2,0,1:T(8,128)} %bitcast.71), calls=%async_computation.2 | async-start | bytes 4194304 | tf_op jit(solution)/shard_map/all_to_all | solution.py:62
  73.6 190.7 %all-gather.13.cloned.1.call-start = ((), (), s32[]{:S(2)}) async-start(), calls=%async_computation.6 | async-start | bytes 2228224 | tf_op jit(solution)/shard_map/all_gather | solution.py:60
  74.3 247.1 %all-gather.11.cloned.1.call-start = ((), (), s32[]{:S(2)}) async-start(), calls=%async_computation.5 | async-start | bytes 2228224 | tf_op jit(solution)/shard_map/all_gather | solution.py:61
  192.7 2.2 copy-start
  218.2 24.0 %collective-permute-start = (f32[2,256,1024]{2,1,0:T(8,128)}, f32[2,256,1024]{2,1,0:T(8,128)S(1)}, u32[]{:S(2)}, u32[]{:S(2)}) collective-permute-start(f32[2,256,1024]{2,1,0:T(8,128)} %copy.79), channel_id=1, source_target_pairs={{0,240},{16,0},{32,16},{48,32},{64,48},{80,64},{96,80},{112,96},{1... | collective-permute-start | bytes 6291464 | tf_op jit(solution)/shard_map/ppermute | solution.py:12
  218.4 217.1 %all-gather.7.cloned.1.call-start = ((), (), s32[]{:S(2)}) async-start(), calls=%async_computation.3 | async-start | bytes 2228224 | tf_op jit(solution)/shard_map/all_gather | solution.py:61
  242.2 1.3 copy-start.1
  277.2 51.8 %collective-permute-start.1 = (f32[2,256,1024]{2,1,0:T(8,128)}, f32[2,256,1024]{2,1,0:T(8,128)S(1)}, u32[]{:S(2)}, u32[]{:S(2)}) collective-permute-start(f32[2,256,1024]{2,1,0:T(8,128)} %get-tuple-element.10), channel_id=1, source_target_pairs={{0,16},{16,32},{32,48},{48,64},{64,80},{80,96},{96,112},{112,128},... | collective-permute-start | bytes 6291464 | tf_op jit(solution)/shard_map/ppermute | solution.py:12
  321.4 114.1 %all-to-all-start.1 = ((f32[1,16,2,32,512]{4,3,2,0,1:T(8,128)}), f32[1,16,2,32,512]{4,3,2,0,1:T(8,128)}, u32[]{:S(2)}, u32[]{:S(2)}) async-start(f32[1,16,2,32,512]{4,3,2,0,1:T(8,128)} %bitcast.72), calls=%async_computation.1 | async-start | bytes 4194304 | tf_op jit(solution)/shard_map/all_to_all | solution.py:62
  329.2 1.6 copy-start.4
  346.4 99.4 %collective-permute-start.2 = (f32[1024,2,256]{2,0,1:T(8,128)}, f32[1024,2,256]{2,0,1:T(8,128)S(1)}, u32[]{:S(2)}, u32[]{:S(2)}) collective-permute-start(f32[1024,2,256]{2,0,1:T(8,128)} %copy.81), channel_id=1, source_target_pairs={{0,15},{1,0},{2,1},{3,2},{4,3},{5,4},{6,5},{7,6},{8,7},{9,8},{10,9... | collective-permute-start | bytes 6291464 | tf_op jit(solution)/shard_map/ppermute | solution.py:12
  435.5 60.6 %all-to-all-start = ((f32[1,16,2,32,512]{4,3,2,0,1:T(8,128)}), f32[1,16,2,32,512]{4,3,2,0,1:T(8,128)}, u32[]{:S(2)}, u32[]{:S(2)}) async-start(f32[1,16,2,32,512]{4,3,2,0,1:T(8,128)} %bitcast.70), calls=%async_computation | async-start | bytes 4194304 | tf_op jit(solution)/shard_map/all_to_all | solution.py:62
  442.1 145.8 %all-gather.9.cloned.1.call-start = ((), (), s32[]{:S(2)}) async-start(), calls=%async_computation.4 | async-start | bytes 2228224 | tf_op jit(solution)/shard_map/all_gather | solution.py:60
  443.3 2.2 copy-start.3
  456.3 92.4 %collective-permute-start.3 = (f32[1024,2,256]{2,0,1:T(8,128)}, f32[1024,2,256]{2,0,1:T(8,128)S(1)}, u32[]{:S(2)}, u32[]{:S(2)}) collective-permute-start(f32[1024,2,256]{2,0,1:T(8,128)} %get-tuple-element.6), channel_id=1, source_target_pairs={{0,1},{1,2},{2,3},{3,4},{4,5},{5,6},{6,7},{7,8},{8,9},{9,10},{10,1... | collective-permute-start | bytes 6291464 | tf_op jit(solution)/shard_map/ppermute | solution.py:12
  548.9 1.6 copy-start.5
  606.1 7.3 %copy-start.2 = (f32[1,1,2,16,32,512]{5,4,3,2,1,0:T(8,128)S(1)}, f32[1,1,2,16,32,512]{5,4,3,2,1,0:T(8,128)}, u32[]{:S(2)}) copy-start(f32[1,1,2,16,32,512]{5,4,3,2,1,0:T(8,128)} %copy.46) | copy-start | bytes 6291460
Sparse Core Ops, SparseCore 0:
  10.1 56.1 all-gather.14
  68.1 99.2 all-gather.16
  169.1 95.1 all-gather.12
  266.9 54.4 all-gather.10
  324.0 111.4 all-gather.6
  444.4 143.4 all-gather.8
where the time goes:
time: 648 us; the launch traced here: 638 us
  waiting for transfers between devices  428 us (66%)
  local copies, waits for them, and re-layouts  98.9 us (15%)
  matrix products  62.3 us (10%)
  starting transfers between devices  28 us (4%)
  between operations  13.9 us (2%)
  other arithmetic  6.62 us (1%)
    all_gather x3, waiting for transfers between devices, local(): gathered = lax.all_gather(chosen, 'row', axis=1, tiled=True)  186 us
    all_gather x3, waiting for transfers between devices, local(): row_raw = lax.all_gather(chosen, 'col', axis=2, tiled=True)[0]  135 us
    ppermute x4, waiting for transfers between devices, passed_along(): return lax.ppermute(value, axis, pairs)  68.3 us
    all_to_all x3, waiting for transfers between devices, local(): lax.all_to_all(sort_columns(gathered, grid_rows), 'col', split_axis=1, co...  36.5 us
    another operation x5, local copies, waits for them, and re-layouts, local(): columns = current.reshape(rows_here, col_blocks, window)  34.2 us
    dot_general x3, matrix products, left_apply(): return jnp.einsum('kab,kan->kbn', factor, stacked, precision=PRECISE)  33.8 us
    dot_general x3, matrix products, right_apply(): return jnp.einsum('nka,kab->nkb', stacked, factor, precision=PRECISE)  28.4 us
    all_to_all x3, starting transfers between devices, local(): lax.all_to_all(sort_columns(gathered, grid_rows), 'col', split_axis=1, co...  21.5 us
  transfers between devices with their start and end apart: 13, of which 9 were waited for; matrix products, arithmetic and copies ran while one was open for 18% of the time, Pallas kernels for 0%

commit v1 on v0

--- a/solution.py
+++ b/solution.py
@@ -4,6 +4,13 @@
 from jax.sharding import PartitionSpec as P
 
 PRECISE = lax.Precision.HIGHEST
+
+
+def exchange_blocks(block, axis, split, join):
+    size = lax.axis_size(axis)
+    blocks = jnp.stack(jnp.split(block, size, axis=split), axis=0)
+    blocks = lax.all_to_all(blocks, axis, split_axis=0, concat_axis=0)
+    return jnp.concatenate(blocks, axis=join)
 
 
 def passed_along(value, axis, steps):
@@ -59,9 +66,7 @@
         chosen = factors[phase_idx : phase_idx + 1]
         row_raw = lax.all_gather(chosen, "col", axis=2, tiled=True)[0]
         gathered = lax.all_gather(chosen, "row", axis=1, tiled=True)
-        col_raw = lax.all_to_all(
-            sort_columns(gathered, grid_rows), "col", split_axis=1, concat_axis=3, tiled=True
-        )
+        col_raw = exchange_blocks(sort_columns(gathered, grid_rows), "col", 1, 3)
         col_raw = col_raw.reshape(col_blocks, window, window)
         flag_all = active[phase_idx]
         row_flag = jnp.take(flag_all, slot_row)

time: 648 us -> 681 us (1.051)
  the two profiles are of different devices: /device:TPU:6 before, /device:TPU:170 now
where the time goes in v1:
time: 681 us; the launch traced here: 670 us
  waiting for transfers between devices  384 us (56%)
  local copies, waits for them, and re-layouts  160 us (23%)
  matrix products  62.1 us (9%)
  starting transfers between devices  43.2 us (6%)
  between operations  14.1 us (2%)
    all_gather x3, waiting for transfers between devices, local(): gathered = lax.all_gather(chosen, 'row', axis=1, tiled=True)  160 us
    ppermute x4, waiting for transfers between devices, passed_along(): return lax.ppermute(value, axis, pairs)  116 us
    all_gather x3, waiting for transfers between devices, local(): row_raw = lax.all_gather(chosen, 'col', axis=2, tiled=True)[0]  86.8 us
    unnamed x70, local copies, waits for them, and re-layouts  74.3 us
    all_to_all x3, starting transfers between devices, exchange_blocks(): blocks = lax.all_to_all(blocks, axis, split_axis=0, concat_axis=0)  35.3 us
    another operation x5, local copies, waits for them, and re-layouts, local(): columns = current.reshape(rows_here, col_blocks, window)  34.3 us
    dot_general x3, matrix products, left_apply(): return jnp.einsum('kab,kan->kbn', factor, stacked, precision=PRECISE)  34 us
    dot_general x3, matrix products, right_apply(): return jnp.einsum('nka,kab->nkb', stacked, factor, precision=PRECISE)  28.1 us
  transfers between devices with their start and end apart: 13, of which 9 were waited for; matrix products, arithmetic and copies ran while one was open for 27% of the time, Pallas kernels for 0%

profile of v1, /device:TPU:170, one launch (start us, length us, event | category | flops | bytes accessed | tf_op | source)
XLA Modules:
  0.0 670.3 jit_solution(674121592610823925)
XLA Ops:
  6.5 1.9 slice_bitcast_fusion.48
  11.1 52.4 %all-gather.15.cloned.1.call-done = f32[1,32,32,512]{3,2,0,1:T(8,128)} async-done(((f32[1,2,32,512]{3,2,0,1:T(8,128)}), f32[1,32,32,512]{3,2,0,1:T(8,128)}) %all-gather.15.cloned.1.call-update) | async-done | bytes 2097168 | tf_op jit(solution)/shard_map/all_gather | solution.py:68
  63.5 1.7 fusion.36
  65.2 1.6 fusion.35
  69.9 1.6 fusion.32
  71.5 1.6 fusion.31
  73.0 1.6 fusion.30
  74.6 1.6 fusion.29
  81.4 8.2 %all-to-all-start.2 = ((f32[16,1,1,2,32,512]{5,4,3,2,1,0:T(8,128)}), f32[16,1,1,2,32,512]{5,4,3,2,1,0:T(8,128)S(1)}, u32[]{:S(2)}, u32[]{:S(2)}) async-start(f32[16,1,1,2,32,512]{5,4,3,2,1,0:T(8,128)} %fusion.21), calls=%async_computation.2 | async-start | bytes 4194304 | tf_op jit(solution)/shard_map/all_to_all | solution.py:12
  92.1 74.6 %all-gather.17.cloned.1.call-done = f32[1,2,512,512]{3,2,1,0:T(8,128)} async-done(((f32[1,2,32,512]{3,2,1,0:T(8,128)}), f32[1,2,512,512]{3,2,1,0:T(8,128)}) %all-gather.17.cloned.1.call-update) | async-done | bytes 2097168 | tf_op jit(solution)/shard_map/all_gather | solution.py:67
  166.7 11.8 %convolution_select_fusion.1 = f32[2,512,1024]{2,1,0:T(8,128)} fusion(f32[2,512,1024]{2,1,0:T(8,128)} %bitcast.249, f32[1,2,512,512]{3,2,1,0:T(8,128)} %all-gather.17.cloned.1.call-done, pred[2,1024]{1,0:T(4,128)(4,1)S(1)} %get-tuple-element.30, f32[512,512]{1,0:T(8,128)S(1)} %fusion.20, pred[2]{0:T(512)(128)(4,1)S(1)} %select_compare_fusion), kind=kOutput, calls=%fused_computation.17 | convolution fusion | flops 6444023808 | bytes 11536386 | tf_op jit(solution)/shard_map/kab,kan->kbn/dot_general | solution.py:23
  178.5 6.6 reshape_reshape.27
  185.1 7.2 %copy.132 = f32[1024,2,512]{0,2,1:T(8,128)} copy(f32[1024,2,512]{2,1,0:T(2,128)} %reshape_reshape.27) | data formatting | bytes 8388608 | tf_op jit(solution)/shard_map/reshape;reshape | solution.py:86
  192.3 33.3 %all-gather.11.cloned.1.call-done = f32[1,32,32,512]{3,2,0,1:T(8,128)} async-done(((f32[1,2,32,512]{3,2,0,1:T(8,128)}), f32[1,32,32,512]{3,2,0,1:T(8,128)}) %all-gather.11.cloned.1.call-update) | async-done | bytes 2097168 | tf_op jit(solution)/shard_map/all_gather | solution.py:68
  225.6 1.6 fusion.52
  228.7 1.6 fusion.50
  230.3 1.6 fusion.49
  232.0 2.0 copy-done
  234.1 8.6 %bitcast_select_fusion.2 = f32[1024,2,512]{0,2,1:T(8,128)} fusion(f32[1024,2,512]{0,2,1:T(8,128)S(1)} %copy-done, f32[2,512,512]{2,1,0:T(8,128)S(1)} %bitcast.247, pred[1024,2]{0,1:T(4,128)(4,1)S(1)} %get-tuple-element.28, f32[512,512]{1,0:T(8,128)S(1)} %fusion.20, pred[2]{0:T(512)(128)(4,1)S(1)} %select_compare_fusion.1), kind=kOutput, calls=%fused_computation.12 | convolution fusion | flops 6444023808 | bytes 11536386 | tf_op jit(solution)/shard_map/nka,kab->nkb/dot_general | solution.py:27
  242.6 6.6 reshape_reshape.28
  249.2 5.0 fusion.78
  254.2 3.0 copy.155
  259.4 1.6 fusion.47
  261.0 1.6 fusion.46
  262.6 1.6 fusion.45
  264.1 1.6 fusion.44
  265.7 1.6 fusion.43
  267.3 1.6 fusion.42
  268.8 1.6 fusion.41
  270.4 1.6 fusion.40
  273.5 4.2 copy.154
  277.7 4.1 collective-permute-done
  283.1 1.9 maximum_select_fusion
  284.9 12.1 %all-gather.13.cloned.1.call-done = f32[1,2,512,512]{3,2,1,0:T(8,128)} async-done(((f32[1,2,32,512]{3,2,1,0:T(8,128)}), f32[1,2,512,512]{3,2,1,0:T(8,128)}) %all-gather.13.cloned.1.call-update) | async-done | bytes 2097168 | tf_op jit(solution)/shard_map/all_gather | solution.py:67
  297.1 10.6 %fusion.1 = f32[2,512,1024]{2,1,0:T(8,128)S(1)} fusion(f32[2,256,1024]{2,1,0:T(8,128)S(1)} %maximum_select_fusion, f32[2,256,1024]{2,1,0:T(8,128)} %copy.154, pred[2,1024]{1,0:T(4,128)(4,1)S(1)} %get-tuple-element.29, f32[1,2,512,512]{3,2,1,0:T(8,128)} %all-gather.13.cloned.1.call-done, f32[512,512]{1,0:T(8,128)S(1)} %fusion.20, pred[2]{0:T(512)(128)(4,1)S(1)} %fusion.70), kind=kOutput, calls=%fused_computation.14 | convolution fusion | flops 6446120960 | bytes 11536386 | tf_op jit(solution)/shard_map/kab,kan->kbn/dot_general | solution.py:23
  307.7 2.3 fusion.77
  310.0 1.6 fusion.38
  313.1 17.9 %all-to-all-start.1 = ((f32[16,1,1,2,32,512]{5,4,3,2,1,0:T(8,128)}), f32[16,1,1,2,32,512]{5,4,3,2,1,0:T(8,128)}, u32[]{:S(2)}, u32[]{:S(2)}) async-start(f32[16,1,1,2,32,512]{5,4,3,2,1,0:T(8,128)} %fusion.37), calls=%async_computation.1 | async-start | bytes 4194304 | tf_op jit(solution)/shard_map/all_to_all | solution.py:12
  331.1 74.7 %all-gather.7.cloned.1.call-done = f32[1,32,32,512]{3,2,0,1:T(8,128)} async-done(((f32[1,2,32,512]{3,2,0,1:T(8,128)}), f32[1,32,32,512]{3,2,0,1:T(8,128)}) %all-gather.7.cloned.1.call-update) | async-done | bytes 2097168 | tf_op jit(solution)/shard_map/all_gather | solution.py:68
  405.8 1.6 fusion.68
  408.9 1.6 fusion.66
  410.4 1.6 fusion.65
  413.5 1.6 fusion.63
  415.1 1.6 fusion.62
  416.7 1.6 fusion.61
  420.0 2.5 pad_maximum_fusion.1
  422.5 6.6 reshape_reshape.29
  429.1 5.0 fusion.76
  442.1 9.2 %all-to-all-start = ((f32[16,1,1,2,32,512]{5,4,3,2,1,0:T(8,128)}), f32[16,1,1,2,32,512]{5,4,3,2,1,0:T(8,128)}, u32[]{:S(2)}, u32[]{:S(2)}) async-start(f32[16,1,1,2,32,512]{5,4,3,2,1,0:T(8,128)} %fusion.53), calls=%async_computation | async-start | bytes 4194304 | tf_op jit(solution)/shard_map/all_to_all | solution.py:12
  452.5 2.0 copy.126
  454.9 59.6 %collective-permute-done.2 = f32[1024,2,256]{2,0,1:T(8,128)S(1)} collective-permute-done((f32[1024,2,256]{2,0,1:T(8,128)}, f32[1024,2,256]{2,0,1:T(8,128)S(1)}, u32[]{:S(2)}, u32[]{:S(2)}) %collective-permute-start.2) | collective-permute-done | bytes 2097184 | tf_op jit(solution)/shard_map/ppermute | solution.py:19
  514.9 7.7 %bitcast_select_fusion.1 = f32[1024,2,512]{2,0,1:T(8,128)S(1)} fusion(f32[1024,2,256]{2,0,1:T(8,128)S(1)} %maximum_select_fusion.2, f32[1024,2,256]{2,0,1:T(8,128)S(1)} %copy.156, pred[1024,2]{0,1:T(4,128)(4,1)S(1)} %get-tuple-element.27, f32[2,512,512]{2,1,0:T(8,128)S(1)} %bitcast.248, f32[512,512]{1,0:T(8,128)S(1)} %fusion.20, pred[2]{0:T(512)(128)(4,1)S(1)} %fusion.69), kind=kOutput, calls=%fused_computation.11 | convolution fusion | flops 6446120960 | bytes 11536386 | tf_op jit(solution)/shard_map/nka,kab->nkb/dot_general | solution.py:27
  522.7 2.4 fusion.75
  525.1 5.9 collective-permute-start.3
  532.3 18.4 %all-to-all-done = f32[16,1,1,2,32,512]{5,4,3,2,1,0:T(8,128)} async-done(((f32[16,1,1,2,32,512]{5,4,3,2,1,0:T(8,128)}), f32[16,1,1,2,32,512]{5,4,3,2,1,0:T(8,128)}, u32[]{:S(2)}, u32[]{:S(2)}) %all-to-all-start) | async-done | bytes 2097184 | tf_op jit(solution)/shard_map/all_to_all | solution.py:12
  550.7 3.2 copy.124
  553.9 52.2 %collective-permute-done.3 = f32[1024,2,256]{2,0,1:T(8,128)S(1)} collective-permute-done((f32[1024,2,256]{2,0,1:T(8,128)}, f32[1024,2,256]{2,0,1:T(8,128)S(1)}, u32[]{:S(2)}, u32[]{:S(2)}) %collective-permute-start.3) | collective-permute-done | bytes 2097184 | tf_op jit(solution)/shard_map/ppermute | solution.py:19
  608.6 5.3 copy.140
  613.8 6.6 reshape_reshape.30
  620.4 11.6 %convolution_select_fusion = f32[2,512,1024]{2,1,0:T(8,128)} fusion(f32[2,512,1024]{2,1,0:T(8,128)} %reshape_reshape.30, f32[1,2,512,512]{3,2,0,1:T(8,128)} %all-gather.9.cloned.1.call-done, pred[2,1024]{1,0:T(4,128)(4,1)S(1)} %get-tuple-element.30, f32[512,512]{1,0:T(8,128)S(1)} %fusion.20, pred[2]{0:T(512)(128)(4,1)S(1)} %select_compare_fusion.2), kind=kOutput, calls=%fused_computation.16 | convolution fusion | flops 6444023808 | bytes 11536386 | tf_op jit(solution)/shard_map/kab,kan->kbn/dot_general | solution.py:23
  632.0 6.6 reshape_reshape.31
  638.6 7.3 %copy.144 = f32[1024,2,512]{0,2,1:T(8,128)} copy(f32[1024,2,512]{2,1,0:T(2,128)} %reshape_reshape.31) | data formatting | bytes 8388608 | tf_op jit(solution)/shard_map/reshape;reshape | solution.py:86
  646.0 11.8 %bitcast_select_fusion = f32[1024,2,512]{0,2,1:T(8,128)} fusion(f32[1024,2,512]{0,2,1:T(8,128)} %copy.144, f32[2,512,512]{2,1,0:T(8,128)S(1)} %bitcast.246, pred[1024,2]{0,1:T(4,128)(4,1)S(1)} %get-tuple-element.28, f32[512,512]{1,0:T(8,128)S(1)} %fusion.20, pred[2]{0:T(512)(128)(4,1)S(1)} %select_compare_fusion.3), kind=kOutput, calls=%fused_computation.10 | convolution fusion | flops 6444023808 | bytes 11536386 | tf_op jit(solution)/shard_map/nka,kab->nkb/dot_general | solution.py:27
  657.8 5.3 copy.145
  (97 shorter events, 40.2 us)
Async XLA Ops:
  6.5 57.0 %all-gather.15.cloned.1.call-start = ((), (), s32[]{:S(2)}) async-start(), calls=%async_computation.7 | async-start | bytes 2228224 | tf_op jit(solution)/shard_map/all_gather | solution.py:68
  8.4 158.2 %all-gather.17.cloned.1.call-start = ((), (), s32[]{:S(2)}) async-start(), calls=%async_computation.8 | async-start | bytes 2228224 | tf_op jit(solution)/shard_map/all_gather | solution.py:67
  9.2 216.4 %all-gather.11.cloned.1.call-start = ((), (), s32[]{:S(2)}) async-start(), calls=%async_computation.5 | async-start | bytes 2228224 | tf_op jit(solution)/shard_map/all_gather | solution.py:68
  9.9 287.1 %all-gather.13.cloned.1.call-start = ((), (), s32[]{:S(2)}) async-start(), calls=%async_computation.6 | async-start | bytes 2228224 | tf_op jit(solution)/shard_map/all_gather | solution.py:67
  10.5 395.2 %all-gather.7.cloned.1.call-start = ((), (), s32[]{:S(2)}) async-start(), calls=%async_computation.3 | async-start | bytes 2228224 | tf_op jit(solution)/shard_map/all_gather | solution.py:68
  63.5 12.6 %copy-start.7 = (f32[1,32,32,512]{3,2,0,1:T(8,128)S(1)}, f32[1,32,32,512]{3,2,0,1:T(8,128)}, u32[]{:S(2)}) copy-start(f32[1,32,32,512]{3,2,0,1:T(8,128)} %all-gather.15.cloned.1.call-done) | copy-start | bytes 6291460
  81.4 8.3 %copy-start.8 = (s32[3,32]{1,0:T(4,128)S(1)}, s32[3,32]{1,0:T(4,128)}, u32[]{:S(2)}) copy-start(s32[3,32]{1,0:T(4,128)} %param.7) | copy-start | bytes 1156
  81.4 150.4 %all-to-all-start.2 = ((f32[16,1,1,2,32,512]{5,4,3,2,1,0:T(8,128)}), f32[16,1,1,2,32,512]{5,4,3,2,1,0:T(8,128)S(1)}, u32[]{:S(2)}, u32[]{:S(2)}) async-start(f32[16,1,1,2,32,512]{5,4,3,2,1,0:T(8,128)} %fusion.21), calls=%async_computation.2 | async-start | bytes 4194304 | tf_op jit(solution)/shard_map/all_to_all | solution.py:12
  231.9 2.2 copy-start
  257.3 24.5 %collective-permute-start = (f32[2,256,1024]{2,1,0:T(8,128)}, f32[2,256,1024]{2,1,0:T(8,128)S(1)}, u32[]{:S(2)}, u32[]{:S(2)}) collective-permute-start(f32[2,256,1024]{2,1,0:T(8,128)} %copy.155), channel_id=1, source_target_pairs={{0,240},{16,0},{32,16},{48,32},{64,48},{80,64},{96,80},{112,96},{1... | collective-permute-start | bytes 6291464 | tf_op jit(solution)/shard_map/ppermute | solution.py:19
  281.8 1.3 copy-start.1
  310.0 108.2 %collective-permute-start.1 = (f32[2,256,1024]{2,1,0:T(8,128)}, f32[2,256,1024]{2,1,0:T(8,128)S(1)}, u32[]{:S(2)}, u32[]{:S(2)}) collective-permute-start(f32[2,256,1024]{2,1,0:T(8,128)} %get-tuple-element.10), channel_id=1, source_target_pairs={{0,16},{16,32},{32,48},{48,64},{64,80},{80,96},{96,112},{112,128},... | collective-permute-start | bytes 6291464 | tf_op jit(solution)/shard_map/ppermute | solution.py:19
  313.1 129.0 %all-to-all-start.1 = ((f32[16,1,1,2,32,512]{5,4,3,2,1,0:T(8,128)}), f32[16,1,1,2,32,512]{5,4,3,2,1,0:T(8,128)}, u32[]{:S(2)}, u32[]{:S(2)}) async-start(f32[16,1,1,2,32,512]{5,4,3,2,1,0:T(8,128)} %fusion.37), calls=%async_computation.1 | async-start | bytes 4194304 | tf_op jit(solution)/shard_map/all_to_all | solution.py:12
  418.4 1.6 copy-start.4
  434.1 2.8 copy-start.6
  435.6 78.9 %collective-permute-start.2 = (f32[1024,2,256]{2,0,1:T(8,128)}, f32[1024,2,256]{2,0,1:T(8,128)S(1)}, u32[]{:S(2)}, u32[]{:S(2)}) collective-permute-start(f32[1024,2,256]{2,0,1:T(8,128)} %copy.157), channel_id=1, source_target_pairs={{0,15},{1,0},{2,1},{3,2},{4,3},{5,4},{6,5},{7,6},{8,7},{9,8},{10,9... | collective-permute-start | bytes 6291464 | tf_op jit(solution)/shard_map/ppermute | solution.py:19
  442.1 108.6 %all-to-all-start = ((f32[16,1,1,2,32,512]{5,4,3,2,1,0:T(8,128)}), f32[16,1,1,2,32,512]{5,4,3,2,1,0:T(8,128)}, u32[]{:S(2)}, u32[]{:S(2)}) async-start(f32[16,1,1,2,32,512]{5,4,3,2,1,0:T(8,128)} %fusion.53), calls=%async_computation | async-start | bytes 4194304 | tf_op jit(solution)/shard_map/all_to_all | solution.py:12
  451.3 169.1 %all-gather.9.cloned.1.call-start = ((), (), s32[]{:S(2)}) async-start(), calls=%async_computation.4 | async-start | bytes 2228224 | tf_op jit(solution)/shard_map/all_gather | solution.py:67
  452.5 2.2 copy-start.2
  525.1 81.1 %collective-permute-start.3 = (f32[1024,2,256]{2,0,1:T(8,128)}, f32[1024,2,256]{2,0,1:T(8,128)S(1)}, u32[]{:S(2)}, u32[]{:S(2)}) collective-permute-start(f32[1024,2,256]{2,0,1:T(8,128)} %get-tuple-element.6), channel_id=1, source_target_pairs={{0,1},{1,2},{2,3},{3,4},{4,5},{5,6},{6,7},{7,8},{8,9},{9,10},{10,1... | collective-permute-start | bytes 6291464 | tf_op jit(solution)/shard_map/ppermute | solution.py:19
  606.3 1.6 copy-start.5
  638.6 7.3 %copy-start.3 = (f32[1,1,2,16,32,512]{5,4,3,2,1,0:T(8,128)S(1)}, f32[1,1,2,16,32,512]{5,4,3,2,1,0:T(8,128)}, u32[]{:S(2)}) copy-start(f32[1,1,2,16,32,512]{5,4,3,2,1,0:T(8,128)} %copy.124) | copy-start | bytes 6291460
Sparse Core Ops, SparseCore 0:
  10.1 53.3 all-gather.14
  65.3 101.3 all-gather.16
  169.4 56.1 all-gather.10
  227.3 69.7 all-gather.12
  299.7 106.0 all-gather.6
  453.6 154.5 all-gather.8
